TPU v7x, 128 devices: a whole 4x4x4 slice. The times are simulated.
128 devices in a mesh: dp: 8 (over y_hi, z), ctx: 16 (over y_lo, x, core).
Axes of the slice: x: 4, y: 4 (y_hi: 2, y_lo: 2; y = y_hi * 2 + y_lo), z: 4, core: 2. Of those that a mesh axis runs over, the one named last changes fastest.
Arguments:
- hidden: bfloat16 [8, 4096, 8192], P('dp', 'ctx'), may hold values from -6 to 6
- queries: bfloat16 [8, 4096, 4096], P('dp', 'ctx')
- layout: int32 [8, 32], P('dp'), may hold values from 0 to 31, each once within a row
- boundary: int32 [8], P('dp'), may hold values from 1 to 4095
- key_matrix: bfloat16 [8192, 512], P(('dp', 'ctx')), may hold values from -0.0625 to 0.0625
- value_matrix: bfloat16 [8192, 512], P(('dp', 'ctx')), may hold values from -0.0625 to 0.0625
Outputs:
- attended: bfloat16 [8, 4096, 4096], P('dp', 'ctx')
Inputs may be any that keep to these rules, and one draw needn't show every extreme that they name: Each row holds every block number of 0 to 31 once; local block b of ctx index c is layout[2 c + b].
All inputs are finite; a program needn't handle non-finite values.
Results may differ from a plain program's by a relative error of at most 0.011.
Values may be sent and summed in bfloat16 or wider, within the bound.
A program may use at most 320 MiB of HBM per device.

v0:
```python
import jax
import jax.numpy as jnp
from jax import lax
from jax.sharding import PartitionSpec as P

HEAD_WIDTH = 128


def shifted(shard, axis, by):
    size = lax.axis_size(axis)
    return lax.ppermute(shard, axis, [(i, (i + by) % size) for i in range(size)])


def per_device(hidden, queries, layout, boundary, key_matrix, value_matrix):
    rows = hidden.shape[1]
    kv_width = key_matrix.shape[1]
    head_size = HEAD_WIDTH
    kv_heads = kv_width // head_size
    group_size = queries.shape[2] // kv_width
    half = rows // 2
    scale = head_size ** (-0.5)
    ctx_count = lax.axis_size("ctx")
    here = lax.axis_index("ctx")
    tokens = hidden[0]
    order = layout[0]
    start_doc = boundary[0]
    block_ids = jnp.arange(order.shape[0], dtype=jnp.int32)

    def positions(first, count):
        index = first + jnp.arange(count, dtype=jnp.int32)
        match = (index // half)[:, None] == block_ids[None, :]
        looked = jnp.sum(jnp.where(match, order[None, :], 0), axis=1)
        return looked * half + index % half

    keys_full = jnp.dot(
        tokens,
        lax.all_gather(key_matrix, ("dp", "ctx"), axis=0, tiled=True),
        preferred_element_type=jnp.float32,
    )
    values_full = jnp.dot(
        tokens,
        lax.all_gather(value_matrix, ("dp", "ctx"), axis=0, tiled=True),
        preferred_element_type=jnp.float32,
    )
    stacked = jnp.stack((keys_full.astype(jnp.bfloat16), values_full.astype(jnp.bfloat16)), axis=0)
    query_rows = queries[0].reshape(rows, kv_heads, group_size, head_size)
    query_pos = positions(here * rows, rows)

    def attend(state, block_list, first):
        count = block_list.shape[1]
        key_pos = positions(first, count)
        allowed = (key_pos[None, :] <= query_pos[:, None]) & (
            (key_pos[None, :] >= start_doc) | (query_pos[:, None] < start_doc)
        )
        running, total, summed = state
        key_row_set = block_list[0].reshape(count, kv_heads, head_size)
        value_row_set = block_list[1].reshape(count, kv_heads, head_size)
        scores = (
            jnp.einsum(
                "qgha,kga->ghqk", query_rows, key_row_set, preferred_element_type=jnp.float32
            )
            * scale
        )
        scores = jnp.where(allowed, scores, -1e30)
        peak = jnp.maximum(running, jnp.max(scores, axis=-1))
        factor = jnp.exp(running - peak)
        weights = jnp.where(allowed, jnp.exp(scores - peak[..., None]), 0.0)
        total = total * factor + jnp.sum(weights, axis=-1)
        probs = weights.astype(jnp.bfloat16)
        summed = summed * factor[..., None] + jnp.einsum(
            "ghqk,kga->ghqa", probs, value_row_set, preferred_element_type=jnp.float32
        )
        return (peak, total, summed)

    initial = (
        jnp.full((kv_heads, group_size, rows), -1e30, jnp.float32),
        jnp.zeros((kv_heads, group_size, rows), jnp.float32),
        jnp.zeros((kv_heads, group_size, rows, head_size), jnp.float32),
    )
    state = attend(initial, stacked, here * rows)

    def turn(step, carry):
        state_now, block_list = carry
        block_list = shifted(block_list, "ctx", 1)
        source = (here - step - 1) % ctx_count
        return (attend(state_now, block_list, source * rows), block_list)

    state, unused_blocks = lax.fori_loop(0, ctx_count - 1, turn, (state, stacked))
    running, total, summed = state
    result = summed / total[..., None]
    result = result.transpose(2, 0, 1, 3).reshape(rows, kv_heads * group_size * head_size)
    return result.astype(jnp.bfloat16)[None]


def solution(mesh):
    in_specs = (
        P("dp", "ctx", None),
        P("dp", "ctx", None),
        P("dp", None),
        P("dp"),
        P(("dp", "ctx"), None),
        P(("dp", "ctx"), None),
    )
    out_specs = P("dp", "ctx", None)
    return jax.shard_map(
        per_device, mesh=mesh, in_specs=in_specs, out_specs=out_specs, check_vma=False
    )
```

profile of v0, /device:TPU:0, one launch (start us, length us, event | category | flops | bytes accessed | tf_op | source)
XLA Modules:
  0.0 751.3 jit_solution(1733711466814543764)
XLA Ops:
  8.7 4.1 copy.26
  12.7 3.0 copy.32
  16.1 198.8 %all-gather.5.cloned.1.call-done = bf16[8192,512]{1,0:T(8,128)(2,1)} async-done(((bf16[64,512]{1,0:T(8,128)(2,1)}), bf16[8192,512]{1,0:T(8,128)(2,1)}) %all-gather.5.cloned.1.call-update) | async-done | bytes 8388624 | tf_op jit(solution)/shard_map/all_gather | solution.py:42
  214.9 7.0 fusion.39
  222.6 195.6 %all-gather.3.cloned.1.call-done = bf16[8192,512]{1,0:T(8,128)(2,1)} async-done(((bf16[64,512]{1,0:T(8,128)(2,1)}), bf16[8192,512]{1,0:T(8,128)(2,1)}) %all-gather.3.cloned.1.call-update) | async-done | bytes 8388624 | tf_op jit(solution)/shard_map/all_gather | solution.py:37
  418.2 7.0 fusion.36
  425.6 3.2 fusion.19
  428.7 2.2 fusion.21
  431.0 4.7 broadcast_add_fusion
  435.7 302.3 %while.23 = (s32[]{:T(128)}, f32[4,8,256]{2,1,0:T(8,128)S(1)}, f32[4,8,256]{2,1,0:T(8,128)S(1)}, f32[4,8,256,128]{3,2,1,0:T(8,128)}, bf16[2,256,512]{1,2,0:T(8,1...) while((s32[]{:T(128)}, f32[4,8,256]{2,1,0:T(8,128)S(1)}, ...), condition=%wide.region_7.8_spmd.clone, body=%wide.region_3.7_spmd.clone.sunk | while | flops 1103347456 | bytes 74720784 | solution.py:88
  436.6 9.8 %collective-permute-done = bf16[2,256,512]{1,2,0:T(8,128)(2,1)S(1)} collective-permute-done((bf16[2,256,512]{1,2,0:T(8,128)(2,1)S(1)}, bf16[2,256,512]{1,2,0:T(8,128)(2,1)S(1)}, u32[]{:S(2)}, u32[]{:S(2)}) %collective-permute-start) | collective-permute-done | bytes 524320 | tf_op jit(solution)/shard_map/while/body/eval_jaxpr/ppermute | solution.py:11
  448.0 2.1 fusion.73
  450.2 3.7 multiply_add_fusion.5
  454.0 1.9 copy-done.1
  456.8 9.8 %collective-permute-done = bf16[2,256,512]{1,2,0:T(8,128)(2,1)S(1)} collective-permute-done((bf16[2,256,512]{1,2,0:T(8,128)(2,1)S(1)}, bf16[2,256,512]{1,2,0:T(8,128)(2,1)S(1)}, u32[]{:S(2)}, u32[]{:S(2)}) %collective-permute-start) | collective-permute-done | bytes 524320 | tf_op jit(solution)/shard_map/while/body/eval_jaxpr/ppermute | solution.py:11
  468.2 2.1 fusion.73
  470.3 3.7 multiply_add_fusion.5
  474.1 1.9 copy-done.1
  476.9 9.8 %collective-permute-done = bf16[2,256,512]{1,2,0:T(8,128)(2,1)S(1)} collective-permute-done((bf16[2,256,512]{1,2,0:T(8,128)(2,1)S(1)}, bf16[2,256,512]{1,2,0:T(8,128)(2,1)S(1)}, u32[]{:S(2)}, u32[]{:S(2)}) %collective-permute-start) | collective-permute-done | bytes 524320 | tf_op jit(solution)/shard_map/while/body/eval_jaxpr/ppermute | solution.py:11
  488.3 2.1 fusion.73
  490.5 3.7 multiply_add_fusion.5
  494.3 1.9 copy-done.1
  497.1 9.8 %collective-permute-done = bf16[2,256,512]{1,2,0:T(8,128)(2,1)S(1)} collective-permute-done((bf16[2,256,512]{1,2,0:T(8,128)(2,1)S(1)}, bf16[2,256,512]{1,2,0:T(8,128)(2,1)S(1)}, u32[]{:S(2)}, u32[]{:S(2)}) %collective-permute-start) | collective-permute-done | bytes 524320 | tf_op jit(solution)/shard_map/while/body/eval_jaxpr/ppermute | solution.py:11
  508.5 2.1 fusion.73
  510.6 3.7 multiply_add_fusion.5
  517.2 9.8 %collective-permute-done = bf16[2,256,512]{1,2,0:T(8,128)(2,1)S(1)} collective-permute-done((bf16[2,256,512]{1,2,0:T(8,128)(2,1)S(1)}, bf16[2,256,512]{1,2,0:T(8,128)(2,1)S(1)}, u32[]{:S(2)}, u32[]{:S(2)}) %collective-permute-start) | collective-permute-done | bytes 524320 | tf_op jit(solution)/shard_map/while/body/eval_jaxpr/ppermute | solution.py:11
  528.6 2.1 fusion.73
  530.8 3.7 multiply_add_fusion.5
  534.6 1.9 copy-done.1
  537.4 9.8 %collective-permute-done = bf16[2,256,512]{1,2,0:T(8,128)(2,1)S(1)} collective-permute-done((bf16[2,256,512]{1,2,0:T(8,128)(2,1)S(1)}, bf16[2,256,512]{1,2,0:T(8,128)(2,1)S(1)}, u32[]{:S(2)}, u32[]{:S(2)}) %collective-permute-start) | collective-permute-done | bytes 524320 | tf_op jit(solution)/shard_map/while/body/eval_jaxpr/ppermute | solution.py:11
  548.8 2.1 fusion.73
  550.9 3.7 multiply_add_fusion.5
  557.5 9.8 %collective-permute-done = bf16[2,256,512]{1,2,0:T(8,128)(2,1)S(1)} collective-permute-done((bf16[2,256,512]{1,2,0:T(8,128)(2,1)S(1)}, bf16[2,256,512]{1,2,0:T(8,128)(2,1)S(1)}, u32[]{:S(2)}, u32[]{:S(2)}) %collective-permute-start) | collective-permute-done | bytes 524320 | tf_op jit(solution)/shard_map/while/body/eval_jaxpr/ppermute | solution.py:11
  568.9 2.1 fusion.73
  571.1 3.7 multiply_add_fusion.5
  574.9 1.9 copy-done.1
  577.7 9.8 %collective-permute-done = bf16[2,256,512]{1,2,0:T(8,128)(2,1)S(1)} collective-permute-done((bf16[2,256,512]{1,2,0:T(8,128)(2,1)S(1)}, bf16[2,256,512]{1,2,0:T(8,128)(2,1)S(1)}, u32[]{:S(2)}, u32[]{:S(2)}) %collective-permute-start) | collective-permute-done | bytes 524320 | tf_op jit(solution)/shard_map/while/body/eval_jaxpr/ppermute | solution.py:11
  589.1 2.1 fusion.73
  591.2 3.7 multiply_add_fusion.5
  597.8 9.8 %collective-permute-done = bf16[2,256,512]{1,2,0:T(8,128)(2,1)S(1)} collective-permute-done((bf16[2,256,512]{1,2,0:T(8,128)(2,1)S(1)}, bf16[2,256,512]{1,2,0:T(8,128)(2,1)S(1)}, u32[]{:S(2)}, u32[]{:S(2)}) %collective-permute-start) | collective-permute-done | bytes 524320 | tf_op jit(solution)/shard_map/while/body/eval_jaxpr/ppermute | solution.py:11
  609.2 2.1 fusion.73
  611.4 3.7 multiply_add_fusion.5
  618.0 9.8 %collective-permute-done = bf16[2,256,512]{1,2,0:T(8,128)(2,1)S(1)} collective-permute-done((bf16[2,256,512]{1,2,0:T(8,128)(2,1)S(1)}, bf16[2,256,512]{1,2,0:T(8,128)(2,1)S(1)}, u32[]{:S(2)}, u32[]{:S(2)}) %collective-permute-start) | collective-permute-done | bytes 524320 | tf_op jit(solution)/shard_map/while/body/eval_jaxpr/ppermute | solution.py:11
  629.4 2.1 fusion.73
  631.6 3.7 multiply_add_fusion.5
  638.1 9.8 %collective-permute-done = bf16[2,256,512]{1,2,0:T(8,128)(2,1)S(1)} collective-permute-done((bf16[2,256,512]{1,2,0:T(8,128)(2,1)S(1)}, bf16[2,256,512]{1,2,0:T(8,128)(2,1)S(1)}, u32[]{:S(2)}, u32[]{:S(2)}) %collective-permute-start) | collective-permute-done | bytes 524320 | tf_op jit(solution)/shard_map/while/body/eval_jaxpr/ppermute | solution.py:11
  649.5 2.1 fusion.73
  651.7 3.7 multiply_add_fusion.5
  658.3 9.8 %collective-permute-done = bf16[2,256,512]{1,2,0:T(8,128)(2,1)S(1)} collective-permute-done((bf16[2,256,512]{1,2,0:T(8,128)(2,1)S(1)}, bf16[2,256,512]{1,2,0:T(8,128)(2,1)S(1)}, u32[]{:S(2)}, u32[]{:S(2)}) %collective-permute-start) | collective-permute-done | bytes 524320 | tf_op jit(solution)/shard_map/while/body/eval_jaxpr/ppermute | solution.py:11
  669.7 2.1 fusion.73
  671.9 3.7 multiply_add_fusion.5
  675.6 1.9 copy-done.1
  678.4 9.8 %collective-permute-done = bf16[2,256,512]{1,2,0:T(8,128)(2,1)S(1)} collective-permute-done((bf16[2,256,512]{1,2,0:T(8,128)(2,1)S(1)}, bf16[2,256,512]{1,2,0:T(8,128)(2,1)S(1)}, u32[]{:S(2)}, u32[]{:S(2)}) %collective-permute-start) | collective-permute-done | bytes 524320 | tf_op jit(solution)/shard_map/while/body/eval_jaxpr/ppermute | solution.py:11
  689.8 2.1 fusion.73
  692.0 3.7 multiply_add_fusion.5
  698.6 9.8 %collective-permute-done = bf16[2,256,512]{1,2,0:T(8,128)(2,1)S(1)} collective-permute-done((bf16[2,256,512]{1,2,0:T(8,128)(2,1)S(1)}, bf16[2,256,512]{1,2,0:T(8,128)(2,1)S(1)}, u32[]{:S(2)}, u32[]{:S(2)}) %collective-permute-start) | collective-permute-done | bytes 524320 | tf_op jit(solution)/shard_map/while/body/eval_jaxpr/ppermute | solution.py:11
  710.0 2.1 fusion.73
  712.2 3.7 multiply_add_fusion.5
  715.9 1.9 copy-done.1
  718.7 9.8 %collective-permute-done = bf16[2,256,512]{1,2,0:T(8,128)(2,1)S(1)} collective-permute-done((bf16[2,256,512]{1,2,0:T(8,128)(2,1)S(1)}, bf16[2,256,512]{1,2,0:T(8,128)(2,1)S(1)}, u32[]{:S(2)}, u32[]{:S(2)}) %collective-permute-start) | collective-permute-done | bytes 524320 | tf_op jit(solution)/shard_map/while/body/eval_jaxpr/ppermute | solution.py:11
  730.2 2.1 fusion.73
  732.3 3.7 multiply_add_fusion.5
  738.0 2.9 fusion.33
  742.2 2.3 convert_element_type.41
  (238 shorter events, 57.4 us)
Async XLA Ops:
  6.5 9.3 %copy-start.3 = (s32[1,32]{1,0:T(1,128)S(1)}, s32[1,32]{1,0:T(1,128)}, u32[]{:S(2)}) copy-start(s32[1,32]{1,0:T(1,128)} %param.10) | copy-start | bytes 388
  6.5 208.3 %all-gather.5.cloned.1.call-start = ((), (), s32[]{:S(2)}) async-start(), calls=%async_computation.1 | async-start | bytes 8454144 | tf_op jit(solution)/shard_map/all_gather | solution.py:42
  7.3 411.0 %all-gather.3.cloned.1.call-start = ((), (), s32[]{:S(2)}) async-start(), calls=%async_computation | async-start | bytes 8454144 | tf_op jit(solution)/shard_map/all_gather | solution.py:37
  425.5 5.4 copy-start.2
  435.7 10.7 %collective-permute-start = (bf16[2,256,512]{1,2,0:T(8,128)(2,1)S(1)}, bf16[2,256,512]{1,2,0:T(8,128)(2,1)S(1)}, u32[]{:S(2)}, u32[]{:S(2)}) collective-permute-start(bf16[2,256,512]{1,2,0:T(8,128)(2,1)S(1)} %get-tuple-element.491), channel_id=1, source_target_pairs={{0,1},{1,2},{2,3},{3,4},{4,5},{5,6},{6,7},{7,8},{8,9},{9,10},{10,1... | collective-permute-start | bytes 1572872 | tf_op jit(solution)/shard_map/while/body/eval_jaxpr/ppermute | solution.py:11
  446.5 3.7 copy-start
  453.9 1.9 copy-start.1
  455.9 10.7 %collective-permute-start = (bf16[2,256,512]{1,2,0:T(8,128)(2,1)S(1)}, bf16[2,256,512]{1,2,0:T(8,128)(2,1)S(1)}, u32[]{:S(2)}, u32[]{:S(2)}) collective-permute-start(bf16[2,256,512]{1,2,0:T(8,128)(2,1)S(1)} %get-tuple-element.491), channel_id=1, source_target_pairs={{0,1},{1,2},{2,3},{3,4},{4,5},{5,6},{6,7},{7,8},{8,9},{9,10},{10,1... | collective-permute-start | bytes 1572872 | tf_op jit(solution)/shard_map/while/body/eval_jaxpr/ppermute | solution.py:11
  466.6 3.7 copy-start
  474.1 1.9 copy-start.1
  476.0 10.7 %collective-permute-start = (bf16[2,256,512]{1,2,0:T(8,128)(2,1)S(1)}, bf16[2,256,512]{1,2,0:T(8,128)(2,1)S(1)}, u32[]{:S(2)}, u32[]{:S(2)}) collective-permute-start(bf16[2,256,512]{1,2,0:T(8,128)(2,1)S(1)} %get-tuple-element.491), channel_id=1, source_target_pairs={{0,1},{1,2},{2,3},{3,4},{4,5},{5,6},{6,7},{7,8},{8,9},{9,10},{10,1... | collective-permute-start | bytes 1572872 | tf_op jit(solution)/shard_map/while/body/eval_jaxpr/ppermute | solution.py:11
  486.8 3.7 copy-start
  494.2 1.9 copy-start.1
  496.2 10.7 %collective-permute-start = (bf16[2,256,512]{1,2,0:T(8,128)(2,1)S(1)}, bf16[2,256,512]{1,2,0:T(8,128)(2,1)S(1)}, u32[]{:S(2)}, u32[]{:S(2)}) collective-permute-start(bf16[2,256,512]{1,2,0:T(8,128)(2,1)S(1)} %get-tuple-element.491), channel_id=1, source_target_pairs={{0,1},{1,2},{2,3},{3,4},{4,5},{5,6},{6,7},{7,8},{8,9},{9,10},{10,1... | collective-permute-start | bytes 1572872 | tf_op jit(solution)/shard_map/while/body/eval_jaxpr/ppermute | solution.py:11
  506.9 3.7 copy-start
  514.4 1.9 copy-start.1
  516.3 10.7 %collective-permute-start = (bf16[2,256,512]{1,2,0:T(8,128)(2,1)S(1)}, bf16[2,256,512]{1,2,0:T(8,128)(2,1)S(1)}, u32[]{:S(2)}, u32[]{:S(2)}) collective-permute-start(bf16[2,256,512]{1,2,0:T(8,128)(2,1)S(1)} %get-tuple-element.491), channel_id=1, source_target_pairs={{0,1},{1,2},{2,3},{3,4},{4,5},{5,6},{6,7},{7,8},{8,9},{9,10},{10,1... | collective-permute-start | bytes 1572872 | tf_op jit(solution)/shard_map/while/body/eval_jaxpr/ppermute | solution.py:11
  527.1 3.7 copy-start
  534.5 1.9 copy-start.1
  536.5 10.7 %collective-permute-start = (bf16[2,256,512]{1,2,0:T(8,128)(2,1)S(1)}, bf16[2,256,512]{1,2,0:T(8,128)(2,1)S(1)}, u32[]{:S(2)}, u32[]{:S(2)}) collective-permute-start(bf16[2,256,512]{1,2,0:T(8,128)(2,1)S(1)} %get-tuple-element.491), channel_id=1, source_target_pairs={{0,1},{1,2},{2,3},{3,4},{4,5},{5,6},{6,7},{7,8},{8,9},{9,10},{10,1... | collective-permute-start | bytes 1572872 | tf_op jit(solution)/shard_map/while/body/eval_jaxpr/ppermute | solution.py:11
  547.2 3.7 copy-start
  554.7 1.9 copy-start.1
  556.6 10.7 %collective-permute-start = (bf16[2,256,512]{1,2,0:T(8,128)(2,1)S(1)}, bf16[2,256,512]{1,2,0:T(8,128)(2,1)S(1)}, u32[]{:S(2)}, u32[]{:S(2)}) collective-permute-start(bf16[2,256,512]{1,2,0:T(8,128)(2,1)S(1)} %get-tuple-element.491), channel_id=1, source_target_pairs={{0,1},{1,2},{2,3},{3,4},{4,5},{5,6},{6,7},{7,8},{8,9},{9,10},{10,1... | collective-permute-start | bytes 1572872 | tf_op jit(solution)/shard_map/while/body/eval_jaxpr/ppermute | solution.py:11
  567.4 3.7 copy-start
  574.8 1.9 copy-start.1
  576.8 10.7 %collective-permute-start = (bf16[2,256,512]{1,2,0:T(8,128)(2,1)S(1)}, bf16[2,256,512]{1,2,0:T(8,128)(2,1)S(1)}, u32[]{:S(2)}, u32[]{:S(2)}) collective-permute-start(bf16[2,256,512]{1,2,0:T(8,128)(2,1)S(1)} %get-tuple-element.491), channel_id=1, source_target_pairs={{0,1},{1,2},{2,3},{3,4},{4,5},{5,6},{6,7},{7,8},{8,9},{9,10},{10,1... | collective-permute-start | bytes 1572872 | tf_op jit(solution)/shard_map/while/body/eval_jaxpr/ppermute | solution.py:11
  587.5 3.7 copy-start
  595.0 1.9 copy-start.1
  596.9 10.7 %collective-permute-start = (bf16[2,256,512]{1,2,0:T(8,128)(2,1)S(1)}, bf16[2,256,512]{1,2,0:T(8,128)(2,1)S(1)}, u32[]{:S(2)}, u32[]{:S(2)}) collective-permute-start(bf16[2,256,512]{1,2,0:T(8,128)(2,1)S(1)} %get-tuple-element.491), channel_id=1, source_target_pairs={{0,1},{1,2},{2,3},{3,4},{4,5},{5,6},{6,7},{7,8},{8,9},{9,10},{10,1... | collective-permute-start | bytes 1572872 | tf_op jit(solution)/shard_map/while/body/eval_jaxpr/ppermute | solution.py:11
  607.7 3.7 copy-start
  615.1 1.9 copy-start.1
  617.1 10.7 %collective-permute-start = (bf16[2,256,512]{1,2,0:T(8,128)(2,1)S(1)}, bf16[2,256,512]{1,2,0:T(8,128)(2,1)S(1)}, u32[]{:S(2)}, u32[]{:S(2)}) collective-permute-start(bf16[2,256,512]{1,2,0:T(8,128)(2,1)S(1)} %get-tuple-element.491), channel_id=1, source_target_pairs={{0,1},{1,2},{2,3},{3,4},{4,5},{5,6},{6,7},{7,8},{8,9},{9,10},{10,1... | collective-permute-start | bytes 1572872 | tf_op jit(solution)/shard_map/while/body/eval_jaxpr/ppermute | solution.py:11
  627.8 3.7 copy-start
  635.3 1.9 copy-start.1
  637.2 10.7 %collective-permute-start = (bf16[2,256,512]{1,2,0:T(8,128)(2,1)S(1)}, bf16[2,256,512]{1,2,0:T(8,128)(2,1)S(1)}, u32[]{:S(2)}, u32[]{:S(2)}) collective-permute-start(bf16[2,256,512]{1,2,0:T(8,128)(2,1)S(1)} %get-tuple-element.491), channel_id=1, source_target_pairs={{0,1},{1,2},{2,3},{3,4},{4,5},{5,6},{6,7},{7,8},{8,9},{9,10},{10,1... | collective-permute-start | bytes 1572872 | tf_op jit(solution)/shard_map/while/body/eval_jaxpr/ppermute | solution.py:11
  648.0 3.7 copy-start
  655.4 1.9 copy-start.1
  657.4 10.7 %collective-permute-start = (bf16[2,256,512]{1,2,0:T(8,128)(2,1)S(1)}, bf16[2,256,512]{1,2,0:T(8,128)(2,1)S(1)}, u32[]{:S(2)}, u32[]{:S(2)}) collective-permute-start(bf16[2,256,512]{1,2,0:T(8,128)(2,1)S(1)} %get-tuple-element.491), channel_id=1, source_target_pairs={{0,1},{1,2},{2,3},{3,4},{4,5},{5,6},{6,7},{7,8},{8,9},{9,10},{10,1... | collective-permute-start | bytes 1572872 | tf_op jit(solution)/shard_map/while/body/eval_jaxpr/ppermute | solution.py:11
  668.1 3.7 copy-start
  675.6 1.9 copy-start.1
  677.5 10.7 %collective-permute-start = (bf16[2,256,512]{1,2,0:T(8,128)(2,1)S(1)}, bf16[2,256,512]{1,2,0:T(8,128)(2,1)S(1)}, u32[]{:S(2)}, u32[]{:S(2)}) collective-permute-start(bf16[2,256,512]{1,2,0:T(8,128)(2,1)S(1)} %get-tuple-element.491), channel_id=1, source_target_pairs={{0,1},{1,2},{2,3},{3,4},{4,5},{5,6},{6,7},{7,8},{8,9},{9,10},{10,1... | collective-permute-start | bytes 1572872 | tf_op jit(solution)/shard_map/while/body/eval_jaxpr/ppermute | solution.py:11
  688.3 3.7 copy-start
  695.7 1.9 copy-start.1
  697.7 10.7 %collective-permute-start = (bf16[2,256,512]{1,2,0:T(8,128)(2,1)S(1)}, bf16[2,256,512]{1,2,0:T(8,128)(2,1)S(1)}, u32[]{:S(2)}, u32[]{:S(2)}) collective-permute-start(bf16[2,256,512]{1,2,0:T(8,128)(2,1)S(1)} %get-tuple-element.491), channel_id=1, source_target_pairs={{0,1},{1,2},{2,3},{3,4},{4,5},{5,6},{6,7},{7,8},{8,9},{9,10},{10,1... | collective-permute-start | bytes 1572872 | tf_op jit(solution)/shard_map/while/body/eval_jaxpr/ppermute | solution.py:11
  708.4 3.7 copy-start
  715.9 1.9 copy-start.1
  717.8 10.7 %collective-permute-start = (bf16[2,256,512]{1,2,0:T(8,128)(2,1)S(1)}, bf16[2,256,512]{1,2,0:T(8,128)(2,1)S(1)}, u32[]{:S(2)}, u32[]{:S(2)}) collective-permute-start(bf16[2,256,512]{1,2,0:T(8,128)(2,1)S(1)} %get-tuple-element.491), channel_id=1, source_target_pairs={{0,1},{1,2},{2,3},{3,4},{4,5},{5,6},{6,7},{7,8},{8,9},{9,10},{10,1... | collective-permute-start | bytes 1572872 | tf_op jit(solution)/shard_map/while/body/eval_jaxpr/ppermute | solution.py:11
  728.6 3.7 copy-start
  736.0 1.9 copy-start.1
Sparse Core Ops, SparseCore 0:
  9.1 205.7 all-gather.4
  216.6 201.5 all-gather.2
where the time goes:
time: 752 us; the launch traced here: 751 us
  waiting for transfers between devices  543 us (72%)
  matrix products  101 us (13%)
  other arithmetic  50.9 us (7%)
  local copies, waits for them, and re-layouts  41.2 us (5%)
  between operations  14.2 us (2%)
    all_gather x1, waiting for transfers between devices, per_device(): lax.all_gather(value_matrix, ('dp', 'ctx'), axis=0, tiled=True)  199 us
    all_gather x1, waiting for transfers between devices, per_device(): lax.all_gather(key_matrix, ('dp', 'ctx'), axis=0, tiled=True)  196 us
    ppermute x15, waiting for transfers between devices, shifted(): lax.ppermute(shard, axis, [(i, (i + by) % size) for i in range(size)])  147 us
    dot_general x16, matrix products, attend(): jnp.einsum('ghqk,kga->ghqa', probs, value_row_set, preferred_element_type...  60.5 us
    reduce_sum x16, other arithmetic, attend(): total = total * factor + jnp.sum(weights, axis=-1)  33.8 us
    while x90, local copies, waits for them, and re-layouts  28.9 us
    dot_general x16, matrix products, attend(): jnp.einsum('qgha,kga->ghqk', query_rows, key_row_set, preferred_element_t...  26.2 us
  transfers between devices with their start and end apart: 17, of which 17 were waited for; matrix products, arithmetic and copies ran while one was open for 4% of the time, Pallas kernels for 0%

commit v1 on v0

--- a/solution.py
+++ b/solution.py
@@ -39,7 +39,12 @@
     )
     values_full = jnp.dot(
         tokens,
-        lax.all_gather(value_matrix, ("dp", "ctx"), axis=0, tiled=True),
+        jnp.concatenate(
+            lax.all_to_all(
+                jnp.stack([value_matrix] * lax.axis_size(("dp", "ctx"))), ("dp", "ctx"), 0, 0
+            ),
+            axis=0,
+        ),
         preferred_element_type=jnp.float32,
     )
     stacked = jnp.stack((keys_full.astype(jnp.bfloat16), values_full.astype(jnp.bfloat16)), axis=0)

time: 752 us -> 635 us (0.84)
  waiting for transfers between devices: 543 us -> 405 us
  starting transfers between devices: 0.08 us -> 11.7 us
    all_gather x1 -> x0, waiting for transfers between devices: 199 us -> none  [per_device(): lax.all_gather(value_matrix, ('dp', 'ctx'), axis=0, tiled=True)]
    all_to_all x0 -> x1, waiting for transfers between devices: none -> 107 us  [per_device(): lax.all_to_all(jnp.stack([value_matrix] * lax.axis_size(('dp', 'ctx'))),...]
    all_gather x1, waiting for transfers between devices: 196 us -> 151 us  [per_device(): lax.all_gather(key_matrix, ('dp', 'ctx'), axis=0, tiled=True)]
    all_to_all x0 -> x1, starting transfers between devices: none -> 11.7 us  [per_device(): lax.all_to_all(jnp.stack([value_matrix] * lax.axis_size(('dp', 'ctx'))),...]
  transfers between devices with their start and end apart: 17 -> 17, of which waited for: 17 -> 17; matrix products, arithmetic and copies ran while one was open for 4% -> 5% of each run, Pallas kernels for 0% -> 0%
where the time goes in v1:
time: 635 us
  waiting for transfers between devices  405 us (64%)
  matrix products  103 us (16%)
  other arithmetic  51.7 us (8%)
  local copies, waits for them, and re-layouts  47.5 us (7%)
  between operations  14.2 us (2%)
  starting transfers between devices  11.7 us (2%)
    all_gather x1, waiting for transfers between devices, per_device(): lax.all_gather(key_matrix, ('dp', 'ctx'), axis=0, tiled=True)  151 us
    ppermute x15, waiting for transfers between devices, shifted(): lax.ppermute(shard, axis, [(i, (i + by) % size) for i in range(size)])  147 us
    all_to_all x1, waiting for transfers between devices, per_device(): lax.all_to_all(jnp.stack([value_matrix] * lax.axis_size(('dp', 'ctx'))),...  107 us
    dot_general x16, matrix products, attend(): jnp.einsum('ghqk,kga->ghqa', probs, value_row_set, preferred_element_type...  63.1 us
    reduce_sum x16, other arithmetic, attend(): total = total * factor + jnp.sum(weights, axis=-1)  34 us
    while x90, local copies, waits for them, and re-layouts  29.2 us
    dot_general x16, matrix products, attend(): jnp.einsum('qgha,kga->ghqk', query_rows, key_row_set, preferred_element_t...  25.7 us
  transfers between devices with their start and end apart: 17, of which 17 were waited for; matrix products, arithmetic and copies ran while one was open for 5% of the time, Pallas kernels for 0%

profile of v1, /device:TPU:0, one launch (start us, length us, event | category | flops | bytes accessed | tf_op | source)
XLA Modules:
  0.0 634.7 jit_solution(11072544672746272154)
XLA Ops:
  7.3 5.1 stack.8
  12.4 11.7 %all-to-all-start = ((bf16[128,64,512]{2,1,0:T(8,128)(2,1)}), bf16[128,64,512]{2,1,0:T(8,128)(2,1)}, u32[]{:S(2)}, u32[]{:S(2)}) async-start(bf16[128,64,512]{2,1,0:T(8,128)(2,1)} %stack.8), calls=%async_computation | async-start | bytes 16777216 | tf_op jit(solution)/shard_map/all_to_all | solution.py:43
  24.7 2.5 copy.26
  27.2 3.0 copy.32
  30.5 107.1 %all-to-all-done = bf16[128,64,512]{2,1,0:T(8,128)(2,1)} async-done(((bf16[128,64,512]{2,1,0:T(8,128)(2,1)}), bf16[128,64,512]{2,1,0:T(8,128)(2,1)}, u32[]{:S(2)}, u32[]{:S(2)}) %all-to-all-start) | async-done | bytes 8388640 | tf_op jit(solution)/shard_map/all_to_all | solution.py:43
  137.6 7.0 %fusion.39 = bf16[256,512]{1,0:T(8,128)(2,1)S(1)} fusion(bf16[8192,512]{1,0:T(8,128)(2,1)} %bitcast.6, bf16[1,256,8192]{2,1,0:T(8,128)(2,1)} %param.8), kind=kOutput, calls=%fused_computation.51 | convolution fusion | flops 2147614720 | bytes 12845056 | tf_op jit(solution)/shard_map/dot_general | solution.py:40
  144.7 150.5 %all-gather.2.cloned.1.call-done = bf16[8192,512]{1,0:T(8,128)(2,1)} async-done(((bf16[64,512]{1,0:T(8,128)(2,1)}), bf16[8192,512]{1,0:T(8,128)(2,1)}) %all-gather.2.cloned.1.call-update) | async-done | bytes 8388624 | tf_op jit(solution)/shard_map/all_gather | solution.py:37
  295.2 7.0 %fusion.36 = bf16[256,512]{1,0:T(8,128)(2,1)S(1)} fusion(bf16[8192,512]{1,0:T(8,128)(2,1)} %all-gather.2.cloned.1.call-done, bf16[1,256,8192]{2,1,0:T(8,128)(2,1)} %param.8), kind=kOutput, calls=%fused_computation.50 | convolution fusion | flops 2147614720 | bytes 12845056 | tf_op jit(solution)/shard_map/dot_general | solution.py:35
  302.3 3.1 fusion.19
  305.4 3.2 copy-done
  308.6 2.1 fusion.21
  311.6 7.0 %broadcast_add_fusion = f32[4,8,256,128]{3,2,1,0:T(8,128)} fusion(f32[4,8,256]{2,1,0:T(8,128)} %get-tuple-element.388, f32[4,256,256,8]{2,1,3,0:T(8,128)} %copy-done, f32[4,8,256]{2,1,0:T(8,128)S(1)} %broadcast_maximum_fusion, pred[256,256]{0,1:T(8,128)(4,1)S(1)} %or_and_fusion.1, bf16[256,4,128,1]{2,1,0,3:T(4,128)(2,1)S(1)} %bitcast.91), kind=kOutput, calls=%fused_computation.48 | convolution fusion | flops 548405248 | bytes 12976128 | tf_op jit(solution)/shard_map/ghqk,kga->ghqa/dot_general | solution.py:75
  318.5 302.8 %while.23 = (s32[]{:T(128)}, f32[4,8,256]{2,1,0:T(8,128)S(1)}, f32[4,8,256]{2,1,0:T(8,128)S(1)}, f32[4,8,256,128]{3,2,1,0:T(8,128)}, bf16[2,256,512]{1,2,0:T(8,1...) while((s32[]{:T(128)}, f32[4,8,256]{2,1,0:T(8,128)S(1)}, ...), condition=%wide.region_7.8_spmd.clone, body=%wide.region_3.7_spmd.clone.sunk | while | flops 1103347456 | bytes 74720784 | solution.py:93
  319.4 9.8 %collective-permute-done = bf16[2,256,512]{1,2,0:T(8,128)(2,1)S(1)} collective-permute-done((bf16[2,256,512]{1,2,0:T(8,128)(2,1)S(1)}, bf16[2,256,512]{1,2,0:T(8,128)(2,1)S(1)}, u32[]{:S(2)}, u32[]{:S(2)}) %collective-permute-start) | collective-permute-done | bytes 524320 | tf_op jit(solution)/shard_map/while/body/eval_jaxpr/ppermute | solution.py:11
  330.8 2.1 fusion.73
  333.0 3.7 multiply_add_fusion.5
  336.8 1.9 copy-done.2
  339.6 9.8 %collective-permute-done = bf16[2,256,512]{1,2,0:T(8,128)(2,1)S(1)} collective-permute-done((bf16[2,256,512]{1,2,0:T(8,128)(2,1)S(1)}, bf16[2,256,512]{1,2,0:T(8,128)(2,1)S(1)}, u32[]{:S(2)}, u32[]{:S(2)}) %collective-permute-start) | collective-permute-done | bytes 524320 | tf_op jit(solution)/shard_map/while/body/eval_jaxpr/ppermute | solution.py:11
  351.0 2.1 fusion.73
  353.2 3.7 multiply_add_fusion.5
  357.0 1.9 copy-done.2
  359.8 9.8 %collective-permute-done = bf16[2,256,512]{1,2,0:T(8,128)(2,1)S(1)} collective-permute-done((bf16[2,256,512]{1,2,0:T(8,128)(2,1)S(1)}, bf16[2,256,512]{1,2,0:T(8,128)(2,1)S(1)}, u32[]{:S(2)}, u32[]{:S(2)}) %collective-permute-start) | collective-permute-done | bytes 524320 | tf_op jit(solution)/shard_map/while/body/eval_jaxpr/ppermute | solution.py:11
  371.2 2.1 fusion.73
  373.4 3.7 multiply_add_fusion.5
  380.0 9.8 %collective-permute-done = bf16[2,256,512]{1,2,0:T(8,128)(2,1)S(1)} collective-permute-done((bf16[2,256,512]{1,2,0:T(8,128)(2,1)S(1)}, bf16[2,256,512]{1,2,0:T(8,128)(2,1)S(1)}, u32[]{:S(2)}, u32[]{:S(2)}) %collective-permute-start) | collective-permute-done | bytes 524320 | tf_op jit(solution)/shard_map/while/body/eval_jaxpr/ppermute | solution.py:11
  391.4 2.1 fusion.73
  393.6 3.7 multiply_add_fusion.5
  397.4 1.9 copy-done.2
  400.2 9.8 %collective-permute-done = bf16[2,256,512]{1,2,0:T(8,128)(2,1)S(1)} collective-permute-done((bf16[2,256,512]{1,2,0:T(8,128)(2,1)S(1)}, bf16[2,256,512]{1,2,0:T(8,128)(2,1)S(1)}, u32[]{:S(2)}, u32[]{:S(2)}) %collective-permute-start) | collective-permute-done | bytes 524320 | tf_op jit(solution)/shard_map/while/body/eval_jaxpr/ppermute | solution.py:11
  411.6 2.1 fusion.73
  413.8 3.7 multiply_add_fusion.5
  417.6 1.9 copy-done.2
  420.4 9.8 %collective-permute-done = bf16[2,256,512]{1,2,0:T(8,128)(2,1)S(1)} collective-permute-done((bf16[2,256,512]{1,2,0:T(8,128)(2,1)S(1)}, bf16[2,256,512]{1,2,0:T(8,128)(2,1)S(1)}, u32[]{:S(2)}, u32[]{:S(2)}) %collective-permute-start) | collective-permute-done | bytes 524320 | tf_op jit(solution)/shard_map/while/body/eval_jaxpr/ppermute | solution.py:11
  431.8 2.1 fusion.73
  433.9 3.7 multiply_add_fusion.5
  440.6 9.8 %collective-permute-done = bf16[2,256,512]{1,2,0:T(8,128)(2,1)S(1)} collective-permute-done((bf16[2,256,512]{1,2,0:T(8,128)(2,1)S(1)}, bf16[2,256,512]{1,2,0:T(8,128)(2,1)S(1)}, u32[]{:S(2)}, u32[]{:S(2)}) %collective-permute-start) | collective-permute-done | bytes 524320 | tf_op jit(solution)/shard_map/while/body/eval_jaxpr/ppermute | solution.py:11
  451.9 2.1 fusion.73
  454.1 3.7 multiply_add_fusion.5
  460.7 9.8 %collective-permute-done = bf16[2,256,512]{1,2,0:T(8,128)(2,1)S(1)} collective-permute-done((bf16[2,256,512]{1,2,0:T(8,128)(2,1)S(1)}, bf16[2,256,512]{1,2,0:T(8,128)(2,1)S(1)}, u32[]{:S(2)}, u32[]{:S(2)}) %collective-permute-start) | collective-permute-done | bytes 524320 | tf_op jit(solution)/shard_map/while/body/eval_jaxpr/ppermute | solution.py:11
  472.1 2.1 fusion.73
  474.3 3.7 multiply_add_fusion.5
  480.9 9.8 %collective-permute-done = bf16[2,256,512]{1,2,0:T(8,128)(2,1)S(1)} collective-permute-done((bf16[2,256,512]{1,2,0:T(8,128)(2,1)S(1)}, bf16[2,256,512]{1,2,0:T(8,128)(2,1)S(1)}, u32[]{:S(2)}, u32[]{:S(2)}) %collective-permute-start) | collective-permute-done | bytes 524320 | tf_op jit(solution)/shard_map/while/body/eval_jaxpr/ppermute | solution.py:11
  492.3 2.1 fusion.73
  494.5 3.7 multiply_add_fusion.5
  501.1 9.8 %collective-permute-done = bf16[2,256,512]{1,2,0:T(8,128)(2,1)S(1)} collective-permute-done((bf16[2,256,512]{1,2,0:T(8,128)(2,1)S(1)}, bf16[2,256,512]{1,2,0:T(8,128)(2,1)S(1)}, u32[]{:S(2)}, u32[]{:S(2)}) %collective-permute-start) | collective-permute-done | bytes 524320 | tf_op jit(solution)/shard_map/while/body/eval_jaxpr/ppermute | solution.py:11
  512.5 2.1 fusion.73
  514.7 3.7 multiply_add_fusion.5
  521.3 9.8 %collective-permute-done = bf16[2,256,512]{1,2,0:T(8,128)(2,1)S(1)} collective-permute-done((bf16[2,256,512]{1,2,0:T(8,128)(2,1)S(1)}, bf16[2,256,512]{1,2,0:T(8,128)(2,1)S(1)}, u32[]{:S(2)}, u32[]{:S(2)}) %collective-permute-start) | collective-permute-done | bytes 524320 | tf_op jit(solution)/shard_map/while/body/eval_jaxpr/ppermute | solution.py:11
  532.7 2.1 fusion.73
  534.9 3.7 multiply_add_fusion.5
  541.5 9.8 %collective-permute-done = bf16[2,256,512]{1,2,0:T(8,128)(2,1)S(1)} collective-permute-done((bf16[2,256,512]{1,2,0:T(8,128)(2,1)S(1)}, bf16[2,256,512]{1,2,0:T(8,128)(2,1)S(1)}, u32[]{:S(2)}, u32[]{:S(2)}) %collective-permute-start) | collective-permute-done | bytes 524320 | tf_op jit(solution)/shard_map/while/body/eval_jaxpr/ppermute | solution.py:11
  552.9 2.1 fusion.73
  555.1 3.7 multiply_add_fusion.5
  561.7 9.8 %collective-permute-done = bf16[2,256,512]{1,2,0:T(8,128)(2,1)S(1)} collective-permute-done((bf16[2,256,512]{1,2,0:T(8,128)(2,1)S(1)}, bf16[2,256,512]{1,2,0:T(8,128)(2,1)S(1)}, u32[]{:S(2)}, u32[]{:S(2)}) %collective-permute-start) | collective-permute-done | bytes 524320 | tf_op jit(solution)/shard_map/while/body/eval_jaxpr/ppermute | solution.py:11
  573.1 2.1 fusion.73
  575.2 3.7 multiply_add_fusion.5
  581.9 9.8 %collective-permute-done = bf16[2,256,512]{1,2,0:T(8,128)(2,1)S(1)} collective-permute-done((bf16[2,256,512]{1,2,0:T(8,128)(2,1)S(1)}, bf16[2,256,512]{1,2,0:T(8,128)(2,1)S(1)}, u32[]{:S(2)}, u32[]{:S(2)}) %collective-permute-start) | collective-permute-done | bytes 524320 | tf_op jit(solution)/shard_map/while/body/eval_jaxpr/ppermute | solution.py:11
  593.2 2.1 fusion.73
  595.4 3.7 multiply_add_fusion.5
  602.1 9.8 %collective-permute-done = bf16[2,256,512]{1,2,0:T(8,128)(2,1)S(1)} collective-permute-done((bf16[2,256,512]{1,2,0:T(8,128)(2,1)S(1)}, bf16[2,256,512]{1,2,0:T(8,128)(2,1)S(1)}, u32[]{:S(2)}, u32[]{:S(2)}) %collective-permute-start) | collective-permute-done | bytes 524320 | tf_op jit(solution)/shard_map/while/body/eval_jaxpr/ppermute | solution.py:11
  613.4 2.1 fusion.73
  615.6 3.7 multiply_add_fusion.5
  621.3 2.9 fusion.33
  625.5 2.3 convert_element_type.41
  (240 shorter events, 62.0 us)
Async XLA Ops:
  6.5 288.7 %all-gather.2.cloned.1.call-start = ((), (), s32[]{:S(2)}) async-start(), calls=%async_computation.1 | async-start | bytes 8454144 | tf_op jit(solution)/shard_map/all_gather | solution.py:37
  12.4 12.4 %copy-start.3 = (bf16[1,256,4096]{2,1,0:T(8,128)(2,1)S(1)}, bf16[1,256,4096]{2,1,0:T(8,128)(2,1)}, u32[]{:S(2)}) copy-start(bf16[1,256,4096]{2,1,0:T(8,128)(2,1)} %param.9) | copy-start | bytes 6291460
  12.4 125.2 %all-to-all-start = ((bf16[128,64,512]{2,1,0:T(8,128)(2,1)}), bf16[128,64,512]{2,1,0:T(8,128)(2,1)}, u32[]{:S(2)}, u32[]{:S(2)}) async-start(bf16[128,64,512]{2,1,0:T(8,128)(2,1)} %stack.8), calls=%async_computation | async-start | bytes 16777216 | tf_op jit(solution)/shard_map/all_to_all | solution.py:43
  24.0 6.2 copy-start.4
  305.3 3.2 copy-start
  318.5 10.7 %collective-permute-start = (bf16[2,256,512]{1,2,0:T(8,128)(2,1)S(1)}, bf16[2,256,512]{1,2,0:T(8,128)(2,1)S(1)}, u32[]{:S(2)}, u32[]{:S(2)}) collective-permute-start(bf16[2,256,512]{1,2,0:T(8,128)(2,1)S(1)} %get-tuple-element.491), channel_id=1, source_target_pairs={{0,1},{1,2},{2,3},{3,4},{4,5},{5,6},{6,7},{7,8},{8,9},{9,10},{10,1... | collective-permute-start | bytes 1572872 | tf_op jit(solution)/shard_map/while/body/eval_jaxpr/ppermute | solution.py:11
  329.3 3.7 copy-start.1
  336.8 2.0 copy-start.2
  338.7 10.7 %collective-permute-start = (bf16[2,256,512]{1,2,0:T(8,128)(2,1)S(1)}, bf16[2,256,512]{1,2,0:T(8,128)(2,1)S(1)}, u32[]{:S(2)}, u32[]{:S(2)}) collective-permute-start(bf16[2,256,512]{1,2,0:T(8,128)(2,1)S(1)} %get-tuple-element.491), channel_id=1, source_target_pairs={{0,1},{1,2},{2,3},{3,4},{4,5},{5,6},{6,7},{7,8},{8,9},{9,10},{10,1... | collective-permute-start | bytes 1572872 | tf_op jit(solution)/shard_map/while/body/eval_jaxpr/ppermute | solution.py:11
  349.5 3.7 copy-start.1
  356.9 2.0 copy-start.2
  358.9 10.7 %collective-permute-start = (bf16[2,256,512]{1,2,0:T(8,128)(2,1)S(1)}, bf16[2,256,512]{1,2,0:T(8,128)(2,1)S(1)}, u32[]{:S(2)}, u32[]{:S(2)}) collective-permute-start(bf16[2,256,512]{1,2,0:T(8,128)(2,1)S(1)} %get-tuple-element.491), channel_id=1, source_target_pairs={{0,1},{1,2},{2,3},{3,4},{4,5},{5,6},{6,7},{7,8},{8,9},{9,10},{10,1... | collective-permute-start | bytes 1572872 | tf_op jit(solution)/shard_map/while/body/eval_jaxpr/ppermute | solution.py:11
  369.7 3.7 copy-start.1
  377.1 2.0 copy-start.2
  379.1 10.7 %collective-permute-start = (bf16[2,256,512]{1,2,0:T(8,128)(2,1)S(1)}, bf16[2,256,512]{1,2,0:T(8,128)(2,1)S(1)}, u32[]{:S(2)}, u32[]{:S(2)}) collective-permute-start(bf16[2,256,512]{1,2,0:T(8,128)(2,1)S(1)} %get-tuple-element.491), channel_id=1, source_target_pairs={{0,1},{1,2},{2,3},{3,4},{4,5},{5,6},{6,7},{7,8},{8,9},{9,10},{10,1... | collective-permute-start | bytes 1572872 | tf_op jit(solution)/shard_map/while/body/eval_jaxpr/ppermute | solution.py:11
  389.8 3.7 copy-start.1
  397.3 2.0 copy-start.2
  399.3 10.7 %collective-permute-start = (bf16[2,256,512]{1,2,0:T(8,128)(2,1)S(1)}, bf16[2,256,512]{1,2,0:T(8,128)(2,1)S(1)}, u32[]{:S(2)}, u32[]{:S(2)}) collective-permute-start(bf16[2,256,512]{1,2,0:T(8,128)(2,1)S(1)} %get-tuple-element.491), channel_id=1, source_target_pairs={{0,1},{1,2},{2,3},{3,4},{4,5},{5,6},{6,7},{7,8},{8,9},{9,10},{10,1... | collective-permute-start | bytes 1572872 | tf_op jit(solution)/shard_map/while/body/eval_jaxpr/ppermute | solution.py:11
  410.0 3.7 copy-start.1
  417.5 2.0 copy-start.2
  419.5 10.7 %collective-permute-start = (bf16[2,256,512]{1,2,0:T(8,128)(2,1)S(1)}, bf16[2,256,512]{1,2,0:T(8,128)(2,1)S(1)}, u32[]{:S(2)}, u32[]{:S(2)}) collective-permute-start(bf16[2,256,512]{1,2,0:T(8,128)(2,1)S(1)} %get-tuple-element.491), channel_id=1, source_target_pairs={{0,1},{1,2},{2,3},{3,4},{4,5},{5,6},{6,7},{7,8},{8,9},{9,10},{10,1... | collective-permute-start | bytes 1572872 | tf_op jit(solution)/shard_map/while/body/eval_jaxpr/ppermute | solution.py:11
  430.2 3.7 copy-start.1
  437.7 2.0 copy-start.2
  439.6 10.7 %collective-permute-start = (bf16[2,256,512]{1,2,0:T(8,128)(2,1)S(1)}, bf16[2,256,512]{1,2,0:T(8,128)(2,1)S(1)}, u32[]{:S(2)}, u32[]{:S(2)}) collective-permute-start(bf16[2,256,512]{1,2,0:T(8,128)(2,1)S(1)} %get-tuple-element.491), channel_id=1, source_target_pairs={{0,1},{1,2},{2,3},{3,4},{4,5},{5,6},{6,7},{7,8},{8,9},{9,10},{10,1... | collective-permute-start | bytes 1572872 | tf_op jit(solution)/shard_map/while/body/eval_jaxpr/ppermute | solution.py:11
  450.4 3.7 copy-start.1
  457.9 2.0 copy-start.2
  459.8 10.7 %collective-permute-start = (bf16[2,256,512]{1,2,0:T(8,128)(2,1)S(1)}, bf16[2,256,512]{1,2,0:T(8,128)(2,1)S(1)}, u32[]{:S(2)}, u32[]{:S(2)}) collective-permute-start(bf16[2,256,512]{1,2,0:T(8,128)(2,1)S(1)} %get-tuple-element.491), channel_id=1, source_target_pairs={{0,1},{1,2},{2,3},{3,4},{4,5},{5,6},{6,7},{7,8},{8,9},{9,10},{10,1... | collective-permute-start | bytes 1572872 | tf_op jit(solution)/shard_map/while/body/eval_jaxpr/ppermute | solution.py:11
  470.6 3.7 copy-start.1
  478.1 2.0 copy-start.2
  480.0 10.7 %collective-permute-start = (bf16[2,256,512]{1,2,0:T(8,128)(2,1)S(1)}, bf16[2,256,512]{1,2,0:T(8,128)(2,1)S(1)}, u32[]{:S(2)}, u32[]{:S(2)}) collective-permute-start(bf16[2,256,512]{1,2,0:T(8,128)(2,1)S(1)} %get-tuple-element.491), channel_id=1, source_target_pairs={{0,1},{1,2},{2,3},{3,4},{4,5},{5,6},{6,7},{7,8},{8,9},{9,10},{10,1... | collective-permute-start | bytes 1572872 | tf_op jit(solution)/shard_map/while/body/eval_jaxpr/ppermute | solution.py:11
  490.8 3.7 copy-start.1
  498.2 2.0 copy-start.2
  500.2 10.7 %collective-permute-start = (bf16[2,256,512]{1,2,0:T(8,128)(2,1)S(1)}, bf16[2,256,512]{1,2,0:T(8,128)(2,1)S(1)}, u32[]{:S(2)}, u32[]{:S(2)}) collective-permute-start(bf16[2,256,512]{1,2,0:T(8,128)(2,1)S(1)} %get-tuple-element.491), channel_id=1, source_target_pairs={{0,1},{1,2},{2,3},{3,4},{4,5},{5,6},{6,7},{7,8},{8,9},{9,10},{10,1... | collective-permute-start | bytes 1572872 | tf_op jit(solution)/shard_map/while/body/eval_jaxpr/ppermute | solution.py:11
  511.0 3.7 copy-start.1
  518.4 2.0 copy-start.2
  520.4 10.7 %collective-permute-start = (bf16[2,256,512]{1,2,0:T(8,128)(2,1)S(1)}, bf16[2,256,512]{1,2,0:T(8,128)(2,1)S(1)}, u32[]{:S(2)}, u32[]{:S(2)}) collective-permute-start(bf16[2,256,512]{1,2,0:T(8,128)(2,1)S(1)} %get-tuple-element.491), channel_id=1, source_target_pairs={{0,1},{1,2},{2,3},{3,4},{4,5},{5,6},{6,7},{7,8},{8,9},{9,10},{10,1... | collective-permute-start | bytes 1572872 | tf_op jit(solution)/shard_map/while/body/eval_jaxpr/ppermute | solution.py:11
  531.1 3.7 copy-start.1
  538.6 2.0 copy-start.2
  540.6 10.7 %collective-permute-start = (bf16[2,256,512]{1,2,0:T(8,128)(2,1)S(1)}, bf16[2,256,512]{1,2,0:T(8,128)(2,1)S(1)}, u32[]{:S(2)}, u32[]{:S(2)}) collective-permute-start(bf16[2,256,512]{1,2,0:T(8,128)(2,1)S(1)} %get-tuple-element.491), channel_id=1, source_target_pairs={{0,1},{1,2},{2,3},{3,4},{4,5},{5,6},{6,7},{7,8},{8,9},{9,10},{10,1... | collective-permute-start | bytes 1572872 | tf_op jit(solution)/shard_map/while/body/eval_jaxpr/ppermute | solution.py:11
  551.3 3.7 copy-start.1
  558.8 2.0 copy-start.2
  560.8 10.7 %collective-permute-start = (bf16[2,256,512]{1,2,0:T(8,128)(2,1)S(1)}, bf16[2,256,512]{1,2,0:T(8,128)(2,1)S(1)}, u32[]{:S(2)}, u32[]{:S(2)}) collective-permute-start(bf16[2,256,512]{1,2,0:T(8,128)(2,1)S(1)} %get-tuple-element.491), channel_id=1, source_target_pairs={{0,1},{1,2},{2,3},{3,4},{4,5},{5,6},{6,7},{7,8},{8,9},{9,10},{10,1... | collective-permute-start | bytes 1572872 | tf_op jit(solution)/shard_map/while/body/eval_jaxpr/ppermute | solution.py:11
  571.5 3.7 copy-start.1
  579.0 2.0 copy-start.2
  581.0 10.7 %collective-permute-start = (bf16[2,256,512]{1,2,0:T(8,128)(2,1)S(1)}, bf16[2,256,512]{1,2,0:T(8,128)(2,1)S(1)}, u32[]{:S(2)}, u32[]{:S(2)}) collective-permute-start(bf16[2,256,512]{1,2,0:T(8,128)(2,1)S(1)} %get-tuple-element.491), channel_id=1, source_target_pairs={{0,1},{1,2},{2,3},{3,4},{4,5},{5,6},{6,7},{7,8},{8,9},{9,10},{10,1... | collective-permute-start | bytes 1572872 | tf_op jit(solution)/shard_map/while/body/eval_jaxpr/ppermute | solution.py:11
  591.7 3.7 copy-start.1
  599.2 2.0 copy-start.2
  601.1 10.7 %collective-permute-start = (bf16[2,256,512]{1,2,0:T(8,128)(2,1)S(1)}, bf16[2,256,512]{1,2,0:T(8,128)(2,1)S(1)}, u32[]{:S(2)}, u32[]{:S(2)}) collective-permute-start(bf16[2,256,512]{1,2,0:T(8,128)(2,1)S(1)} %get-tuple-element.491), channel_id=1, source_target_pairs={{0,1},{1,2},{2,3},{3,4},{4,5},{5,6},{6,7},{7,8},{8,9},{9,10},{10,1... | collective-permute-start | bytes 1572872 | tf_op jit(solution)/shard_map/while/body/eval_jaxpr/ppermute | solution.py:11
  611.9 3.7 copy-start.1
  619.4 2.0 copy-start.2
Sparse Core Ops, SparseCore 0:
  9.1 286.0 all-gather.1
